TPU v7x, 32 devices: a whole 2x2x4 slice. The times are simulated.
32 devices in a mesh: seq: 8 (over z, y), head: 4 (over x, core).
Axes of the slice: x: 2, y: 2, z: 4, core: 2. Of those that a mesh axis runs over, the one named last changes fastest.
Arguments:
- query: bfloat16 [8192, 4096], P('seq', 'head'), may hold values from -0.15625 to 0.15625
- key: bfloat16 [8192, 4096], P('seq', 'head'), may hold values from -0.15625 to 0.15625
- value: bfloat16 [8192, 4096], P('seq', 'head'), may hold values from -18 to 18, as said below
- level_coef: float32 [4, 32, 8192], P(None, 'head', 'seq'), may hold values from 0.25 to 2.5
- gain: float32 [4096], P('head'), may hold values from 0.5 to 1.5
- cotangent: bfloat16 [8192, 4096], P('seq', 'head'), may hold values from -0.625 to 0.625
Outputs:
- mixed: bfloat16 [8192, 4096], P('seq', 'head')
- grad_query: bfloat16 [8192, 4096], P('seq', 'head')
- grad_key: bfloat16 [8192, 4096], P('seq', 'head')
- grad_value: bfloat16 [8192, 4096], P('seq', 'head')
- grad_level: float32 [4, 32, 8192], P(None, 'head', 'seq')
- grad_gain: float32 [4096], P('head')
Inputs may be any that keep to these rules, and one draw needn't show every extreme that they name: `value`: real values.
All inputs are finite; a program needn't handle non-finite values.
Results may differ from a plain program's by a relative error of at most 0.0065.
Values sent between devices are 32-bit elements; how exact they have to be, the bound alone decides.
No kernel may reach another device: no remote copies, remote signals or barrier semaphores. Data moves between devices by JAX's collectives and lax.ppermute only.
A program may use at most 128 MiB of HBM per device.

v0:
```python
import jax
import jax.numpy as jnp
from jax import lax
from jax.sharding import PartitionSpec as P

HEADS = 32
HEAD_DIM = 128
EPS = 1e-06


def from_partner(block, axis, apart):
    count = lax.axis_size(axis)
    route = []
    for low in range(count):
        high = low | 1 << apart
        if high != low and high < count:
            route += [(low, high), (high, low)]
    return lax.ppermute(block, axis, route)


def body(query, key, value, level_coef, gain, cotangent):
    f32 = jnp.float32
    bf16 = jnp.bfloat16
    rows = query.shape[0]
    heads_here = level_coef.shape[1]
    width = query.shape[1] // heads_here
    depth = level_coef.shape[0] - 1
    group = lax.axis_index("seq")
    q_three = query.reshape(rows, heads_here, width)
    k_three = key.reshape(rows, heads_here, width)
    v_three = value.reshape(rows, heads_here, width)
    scores = jnp.einsum("the,she->hts", q_three, k_three, preferred_element_type=f32)
    causal = lax.broadcasted_iota(jnp.int32, (rows, rows), 0) >= lax.broadcasted_iota(
        jnp.int32, (rows, rows), 1
    )
    kept = jnp.where(causal[None], scores, 0.0).astype(bf16)
    local = jnp.einsum("hts,she->the", kept, v_three, preferred_element_type=f32)
    states = jnp.einsum("sha,shb->hab", k_three, v_three, preferred_element_type=f32)
    bits = [(group // 2**level % 2).astype(f32) for level in range(depth)]
    block = states
    found = []
    for level in range(depth):
        other = from_partner(block, "seq", level)
        found.append(bits[level] * other)
        block = block + other
    buckets = jnp.stack(found)
    bucket_half = buckets.astype(bf16)
    reads = jnp.einsum("the,lhef->lthf", q_three, bucket_half, preferred_element_type=f32)
    first = level_coef[0].T[:, :, None]
    rest = level_coef[1:].transpose(0, 2, 1)[..., None]
    output = first * local + jnp.sum(rest * reads, axis=0)
    squares = lax.psum(jnp.sum(output * output, axis=(1, 2)), "head")
    scale = lax.rsqrt(squares / (HEADS * HEAD_DIM) + EPS)[:, None, None]
    normed = output * scale
    gain_three = gain.reshape(heads_here, width)
    mixed = (normed * gain_three).astype(bf16).reshape(rows, -1)
    cot_three = cotangent.reshape(rows, heads_here, width).astype(f32)
    grad_gain = lax.psum(jnp.sum(cot_three * normed, axis=0).reshape(-1), "seq")
    weighted_cot = cot_three * gain_three
    inner = lax.psum(jnp.sum(weighted_cot * output, axis=(1, 2)), "head")
    grad_full = (
        weighted_cot - output * (inner[:, None, None] * scale * scale / (HEADS * HEAD_DIM))
    ) * scale
    grad_half = grad_full.astype(bf16)
    grad_float = grad_half.astype(f32)
    grad_first = jnp.sum(grad_float * local, axis=-1)
    grad_rest = jnp.sum(grad_float[None] * reads, axis=-1)
    grad_level = jnp.concatenate([grad_first.T[None], grad_rest.transpose(0, 2, 1)], axis=0)
    weighted = (first * grad_float).astype(bf16)
    value_sum = jnp.einsum("hts,the->she", kept, weighted, preferred_element_type=f32)
    pair = (
        jnp.einsum("the,she->hts", grad_half, v_three, preferred_element_type=f32)
        * level_coef[0][:, :, None]
    )
    pair = jnp.where(causal[None], pair, 0.0).astype(bf16)
    query_sum = jnp.einsum("hts,she->the", pair, k_three, preferred_element_type=f32)
    key_sum = jnp.einsum("hts,the->she", pair, q_three, preferred_element_type=f32)
    scaled = (rest * grad_float[None]).astype(bf16)
    query_sum = query_sum + jnp.einsum(
        "lthf,lhef->the", scaled, bucket_half, preferred_element_type=f32
    )
    grad_buckets = jnp.einsum("the,lthf->lhef", q_three, scaled, preferred_element_type=f32)
    masks = jnp.stack(bits)[:, None, None, None]
    pending = masks * grad_buckets
    carried = jnp.zeros_like(states)
    for level in range(depth):
        other = from_partner(pending, "seq", level)
        carried = carried + (1.0 - bits[level]) * other[0]
        pending = pending[1:] + other[1:]
    grad_states = carried.astype(bf16)
    key_sum = key_sum + jnp.einsum("shb,hab->sha", v_three, grad_states, preferred_element_type=f32)
    value_sum = value_sum + jnp.einsum(
        "sha,hab->shb", k_three, grad_states, preferred_element_type=f32
    )
    grad_query = query_sum.astype(bf16).reshape(rows, -1)
    grad_key = key_sum.astype(bf16).reshape(rows, -1)
    grad_value = value_sum.astype(bf16).reshape(rows, -1)
    return (mixed, grad_query, grad_key, grad_value, grad_level, grad_gain)


def solution(mesh):
    placed = (
        P("seq", "head"),
        P("seq", "head"),
        P("seq", "head"),
        P(None, "head", "seq"),
        P("head"),
        P("seq", "head"),
    )
    return jax.shard_map(
        body,
        mesh=mesh,
        in_specs=placed,
        out_specs=(
            P("seq", "head"),
            P("seq", "head"),
            P("seq", "head"),
            P("seq", "head"),
            P(None, "head", "seq"),
            P("head"),
        ),
        check_vma=False,
    )
```

profile of v0, /device:TPU:0, one launch (start us, length us, event | category | flops | bytes accessed | tf_op | source)
XLA Modules:
  0.0 245.2 jit_solution(4690820925191589461)
XLA Ops:
  0.6 3.7 %copy.75 = bf16[128,8,8,128]{3,2,1,0:T(8,128)(2,1)} copy(bf16[128,8,8,128]{3,1,2,0:T(8,128)(2,1)} %bitcast.130) | data formatting | bytes 4194304
  4.3 4.1 %copy.39 = bf16[1024,8,128]{0,2,1:T(8,128)(2,1)} copy(bf16[1024,8,128]{2,1,0:T(8,128)(2,1)} %bitcast.129) | data formatting | bytes 4194304 | tf_op jit(solution)/shard_map/reshape | solution.py:30
  8.4 2.3 fusion.15
  10.8 3.1 %collective-permute-start = (f32[8,128,128]{2,1,0:T(8,128)S(1)}, f32[8,128,128]{2,1,0:T(8,128)}, u32[]{:S(2)}, u32[]{:S(2)}) collective-permute-start(f32[8,128,128]{2,1,0:T(8,128)S(1)} %fusion.15), channel_id=1, source_target_pairs={{0,4},{4,0},{8,12},{12,8},{16,20},{20,16},{24,28},{28,24},{1,5},{5... | collective-permute-start | bytes 1572872 | tf_op jit(solution)/shard_map/ppermute | solution.py:18
  13.9 3.5 %copy.74 = bf16[128,8,8,128]{3,2,1,0:T(8,128)(2,1)} copy(bf16[128,8,8,128]{3,1,2,0:T(8,128)(2,1)} %bitcast.133) | data formatting | bytes 4194304
  17.4 4.1 %copy.49 = bf16[1024,8,128]{0,2,1:T(8,128)(2,1)} copy(bf16[1024,8,128]{2,1,0:T(8,128)(2,1)} %bitcast.122) | data formatting | bytes 4194304 | tf_op jit(solution)/shard_map/reshape | solution.py:29
  21.8 4.1 %collective-permute-done = f32[8,128,128]{2,1,0:T(8,128)} collective-permute-done((f32[8,128,128]{2,1,0:T(8,128)S(1)}, f32[8,128,128]{2,1,0:T(8,128)}, u32[]{:S(2)}, u32[]{:S(2)}) %collective-permute-start) | collective-permute-done | bytes 524320 | tf_op jit(solution)/shard_map/ppermute | solution.py:18
  25.9 1.3 fusion.37
  27.2 1.9 collective-permute-start.1
  29.1 10.4 %select_convert_fusion.1 = bf16[8,1024,1024]{2,1,0:T(8,128)(2,1)} fusion(pred[1024,1024]{1,0:T(8,128)(4,1)S(1)} %iota_compare_fusion, bf16[1024,8,128]{0,2,1:T(8,128)(2,1)} %copy.49, bf16[1024,1024]{1,0:T(8,128)(2,1)} %param.7), kind=kOutput, calls=%fused_computation.1 | convolution fusion | flops 2164260864 | bytes 22020096 | tf_op jit(solution)/shard_map/the,she->hts/dot_general | solution.py:32
  39.4 1.0 collective-permute-done.1
  40.4 1.9 fusion.38
  42.4 2.5 %collective-permute-start.2 = (f32[8,128,128]{2,1,0:T(8,128)}, f32[8,128,128]{2,1,0:T(8,128)}, u32[]{:S(2)}, u32[]{:S(2)}) collective-permute-start(f32[8,128,128]{2,1,0:T(8,128)} %get-tuple-element.30), channel_id=1, source_target_pairs={{0,16},{16,0},{4,20},{20,4},{8,24},{24,8},{12,28},{28,12},{1,17},{... | collective-permute-start | bytes 1572872 | tf_op jit(solution)/shard_map/ppermute | solution.py:18
  45.0 4.1 %copy.43 = f32[1024,1024]{0,1:T(8,128)} copy(bf16[1024,1024]{1,0:T(8,128)(2,1)} %param.11) | data formatting | bytes 6291456 | tf_op jit(solution)/shard_map/convert_element_type | solution.py:57
  49.2 17.9 %collective-permute-done.2 = f32[8,128,128]{2,1,0:T(8,128)} collective-permute-done((f32[8,128,128]{2,1,0:T(8,128)}, f32[8,128,128]{2,1,0:T(8,128)}, u32[]{:S(2)}, u32[]{:S(2)}) %collective-permute-start.2) | collective-permute-done | bytes 524320 | tf_op jit(solution)/shard_map/ppermute | solution.py:18
  67.0 1.1 fusion.39
  68.1 10.4 %fusion = (f32[1024,8,128]{0,2,1:T(8,128)}, f32[8,3,128,1024]{3,2,1,0:T(8,128)}) fusion(f32[3,1024,8]{1,0,2:T(4,128)S(1)} %copy.38, bf16[1024,8,128,1]{2,1,0,3:T(8,128)(2,1)} %bitcast.123, bf16[1,8,128,128]{3,2,1,0:T(8,128)(2,1)S(1)} %fusion.39, bf16[1,8,128,128]{3,2,1,0:T(8,128)(2,1)S(1)} %get-tuple-element.29, ...), kind=kOutput, calls=%fused_computation.4 | convolution fusion | flops 811335680 | bytes 19759104 | tf_op jit(solution)/shard_map/the,lhef->lthf/dot_general | solution.py:48
  78.5 12.1 %multiply_reduce_fusion.2 = (f32[1024]{0:T(1024)S(1)}, f32[1024,8,128]{0,2,1:T(8,128)}, f32[8,1024,128]{1,2,0:T(8,128)}) fusion(f32[1024,8,128]{0,2,1:T(8,128)} %get-tuple-element.33, f32[1024,8]{0,1:T(8,128)S(1)} %get-tuple-element.32, bf16[8,1024,1024]{2,1,0:T(8,128)(2,1)} %select_convert_fusion.1, bf16[1024,1024]{1,0:T(8,128)(2,1)S(1)} %copy-done), kind=kOutput, calls=%fused_computation.23 | convolution fusion | flops 2151676928 | bytes 31494144 | tf_op jit(solution)/shard_map/hts,she->the/dot_general | solution.py:37
  90.6 5.6 %psum.21 = f32[1024]{0:T(1024)S(1)} all-reduce(f32[1024]{0:T(1024)S(1)} %get-tuple-element.22), channel_id=1, replica_groups=mesh['seq'=8,'head'=4] {'head'}, use_global_device_ids=true, to_apply=%region_2.3 | all-reduce | flops 1024 | bytes 8192 | tf_op jit(solution)/shard_map/psum | solution.py:52
  96.2 5.7 %multiply_reduce_fusion = (f32[8,128]{1,0:T(8,128)S(1)}, f32[1024]{0:T(1024)S(1)}) fusion(f32[1024,8,128]{0,2,1:T(8,128)} %bitcast.121, f32[1024,8,128]{0,2,1:T(8,128)} %get-tuple-element.23, f32[1024]{0:T(1024)S(1)} %add_rsqrt_fusion, f32[8,128]{1,0:T(8,128)S(1)} %bitcast.136, f32[1024,1024]{0,1:T(8,128)} %copy.43), kind=kLoop, calls=%fused_computation.17 | loop fusion | flops 6289408 | bytes 12599296 | tf_op jit(solution)/shard_map/reduce_sum | solution.py:58
  101.9 6.5 %psum.22 = f32[1024]{0:T(1024)S(1)} all-reduce(f32[1024]{0:T(1024)S(1)} %get-tuple-element.19), channel_id=1, replica_groups=mesh['seq'=8,'head'=4] {'head'}, use_global_device_ids=true, to_apply=%region_4.5 | all-reduce | flops 1024 | bytes 8192 | tf_op jit(solution)/shard_map/psum | solution.py:60
  108.5 6.7 %fusion.7 = (f32[1024,8]{0,1:T(8,128)S(1)}, bf16[1024,8,128]{0,2,1:T(8,128)(2,1)S(1)}, bf16[1024,8,128]{0,2,1:T(8,128)(2,1)}) fusion(f32[8,1024,128]{1,2,0:T(8,128)} %get-tuple-element.35, f32[1024]{0:T(1024)S(1)} %add_rsqrt_fusion, f32[1024,8,128]{0,2,1:T(8,128)} %get-tuple-element.23, f32[1024]{0:T(1024)S(1)} %fusion.41, f32[8,128]{1,0:T(8,128)S(1)} %bitcast.137, ...), kind=kLoop, calls=%fused_computation.16 | loop fusion | flops 11526144 | bytes 16822272 | tf_op jit(solution)/shard_map/reduce_sum | solution.py:66
  115.2 0.4 convert_element_type.64
  115.7 1.0 slice-done.1
  116.7 1.6 slice-done.2
  118.3 4.3 %fusion.1 = (f32[3,1024,8]{1,0,2:T(4,128)S(1)}, bf16[3,1024,8,128]{1,3,0,2:T(8,128)(2,1)}) fusion(f32[8,3,128,1024]{3,2,1,0:T(8,128)S(1)} %bitcast.118, f32[1024,8,128]{0,2,1:T(8,128)S(1)} %convert_element_type.64, f32[3,1024,8]{1,0,2:T(4,128)S(1)} %copy.38), kind=kLoop, calls=%fused_computation.5 | loop fusion | flops 12558336 | bytes 23265280 | tf_op jit(solution)/shard_map/reduce_sum | solution.py:67
  122.7 0.7 copy.58
  123.4 3.0 %multiply_bitcast_fusion = f32[3,8,128,128]{2,3,0,1:T(8,128)} fusion(bf16[1024,8,128,1]{2,1,0,3:T(8,128)(2,1)S(1)} %bitcast.124, f32[3]{0:T(128)S(1)} %pad_maximum_fusion.2, f32[1024,8,128]{0,2,1:T(8,128)S(1)} %convert_element_type.64, f32[3,1024,8]{1,0,2:T(4,128)S(1)} %copy.38), kind=kOutput, calls=%fused_computation.42 | convolution fusion | flops 811991040 | bytes 7962636 | tf_op jit(solution)/shard_map/the,lthf->lhef/dot_general | solution.py:82
  126.4 1.3 collective-permute-start.3
  127.6 9.6 %select_convert_fusion = bf16[8,1024,1024]{2,1,0:T(8,128)(2,1)} fusion(f32[8,1024]{1,0:T(8,128)S(1)} %get-tuple-element.31, pred[1024,1024]{1,0:T(8,128)(4,1)S(1)} %copy-done.4, bf16[1024,8,128]{0,2,1:T(8,128)(2,1)S(1)} %get-tuple-element.21, bf16[1024,1024]{1,0:T(8,128)(2,1)S(1)} %copy-done), kind=kOutput, calls=%fused_computation | convolution fusion | flops 2172649472 | bytes 22052864 | tf_op jit(solution)/shard_map/the,she->hts/dot_general | solution.py:72
  137.3 11.4 %fusion.43 = f32[8,1024,128]{1,2,0:T(8,128)} fusion(bf16[8,1024,1024]{2,1,0:T(8,128)(2,1)} %select_convert_fusion, bf16[1024,8,128]{0,2,1:T(8,128)(2,1)} %copy.39), kind=kOutput, calls=%fused_computation.71 | convolution fusion | flops 2147483648 | bytes 23068672 | tf_op jit(solution)/shard_map/hts,she->the/dot_general | solution.py:76
  148.7 10.9 %fusion.10 = f32[8,128,1024]{2,1,0:T(8,128)} fusion(bf16[8,1024,1024]{2,1,0:T(8,128)(2,1)} %select_convert_fusion.1, bf16[1024,8,128]{0,2,1:T(8,128)(2,1)} %copy-done.2, f32[1024,8]{0,1:T(8,128)S(1)} %get-tuple-element.32), kind=kOutput, calls=%fused_computation.25 | convolution fusion | flops 2150629376 | bytes 23101440 | tf_op jit(solution)/shard_map/hts,the->she/dot_general | solution.py:70
  159.6 2.4 collective-permute-done.3
  162.0 2.8 %slice_add_fusion = f32[2,8,128,128]{2,3,0,1:T(8,128)} fusion(f32[3,8,128,128]{2,3,0,1:T(8,128)} %collective-permute-done.3, f32[3,8,128,128]{2,3,0,1:T(8,128)} %multiply_bitcast_fusion), kind=kLoop, calls=%fused_computation.47 | loop fusion | flops 262144 | bytes 3145728 | tf_op jit(solution)/shard_map/add | solution.py:89
  164.8 1.5 collective-permute-start.4
  166.3 6.1 %fusion.44 = f32[8,1024,128]{1,2,0:T(8,128)} fusion(bf16[1024,8,128]{0,2,1:T(8,128)(2,1)} %copy.49, bf16[8,1024,1024]{2,1,0:T(8,128)(2,1)S(1)} %bitcast.120), kind=kOutput, calls=%fused_computation.72 | convolution fusion | flops 2147483648 | bytes 23068672 | tf_op jit(solution)/shard_map/hts,the->she/dot_general | solution.py:77
  172.4 16.3 %collective-permute-done.4 = f32[2,8,128,128]{2,3,0,1:T(8,128)} collective-permute-done((f32[2,8,128,128]{2,3,0,1:T(8,128)}, f32[2,8,128,128]{2,3,0,1:T(8,128)}, u32[]{:S(2)}, u32[]{:S(2)}) %collective-permute-start.4) | collective-permute-done | bytes 1048608 | tf_op jit(solution)/shard_map/ppermute | solution.py:18
  188.7 1.3 slice_add_fusion.1
  190.0 3.4 %collective-permute-start.5 = (f32[1,8,128,128]{2,3,0,1:T(8,128)S(1)}, f32[1,8,128,128]{2,3,0,1:T(8,128)}, u32[]{:S(2)}, u32[]{:S(2)}) collective-permute-start(f32[1,8,128,128]{2,3,0,1:T(8,128)S(1)} %slice_add_fusion.1), channel_id=1, source_target_pairs={{0,16},{16,0},{4,20},{20,4},{8,24},{24,8},{12,28},{28,12},{1,17},{... | collective-permute-start | bytes 1572872 | tf_op jit(solution)/shard_map/ppermute | solution.py:18
  193.4 4.8 %fusion.4 = bf16[1024,8,128]{0,2,1:T(8,128)(2,1)} fusion(f32[8,1024,128]{1,2,0:T(8,128)} %fusion.43, bf16[3,1024,8,128]{1,3,0,2:T(8,128)(2,1)S(1)} %bitcast.126, bf16[1,8,128,128]{3,2,1,0:T(8,128)(2,1)S(1)} %fusion.39, bf16[1,8,128,128]{3,2,1,0:T(8,128)(2,1)S(1)} %get-tuple-element.29, bf16[1,8,128,128]{3,2,1,0:T(8,128)(2,1)S(1)} %get-tuple-element.27), kind=kOutput, calls=%fused_computation.10 | convolution fusion | flops 808189952 | bytes 13369344 | tf_op jit(solution)/shard_map/lthf,lhef->the/dot_general | solution.py:79
  198.2 3.9 %copy.55 = bf16[1024,1024]{1,0:T(8,128)(2,1)} copy(bf16[1024,1024]{0,1:T(8,128)(2,1)} %bitcast.128) | data formatting | bytes 4194304
  202.1 3.9 %copy.54 = bf16[1024,1024]{1,0:T(8,128)(2,1)} copy(bf16[1024,1024]{0,1:T(8,128)(2,1)} %bitcast.127) | data formatting | bytes 4194304
  206.0 20.6 %psum.23 = f32[1024]{0:T(1024)} all-reduce(f32[1024]{0:T(1024)S(1)} %bitcast.138), channel_id=1, replica_groups=mesh['seq'=8,'head'=4] {'seq'}, use_global_device_ids=true, to_apply=%region_8.9 | all-reduce | flops 1024 | bytes 8192 | tf_op jit(solution)/shard_map/psum | solution.py:58
  226.6 1.5 fusion.40
  228.1 4.9 %add_convert_fusion = bf16[8,128,1024]{2,1,0:T(8,128)(2,1)} fusion(f32[8,128,1024]{2,1,0:T(8,128)} %fusion.10, bf16[8,128,128]{1,2,0:T(8,128)(2,1)S(1)} %fusion.40, bf16[1024,1024]{1,0:T(8,128)(2,1)} %param.7), kind=kOutput, calls=%fused_computation.18 | convolution fusion | flops 270532608 | bytes 8650752 | tf_op jit(solution)/shard_map/sha,hab->shb/dot_general | solution.py:92
  233.0 3.9 %copy.57 = bf16[1024,1024]{1,0:T(8,128)(2,1)} copy(bf16[1024,1024]{0,1:T(8,128)(2,1)} %bitcast.132) | data formatting | bytes 4194304
  236.9 4.3 %fusion.5 = bf16[1024,8,128]{0,2,1:T(8,128)(2,1)} fusion(f32[8,1024,128]{1,2,0:T(8,128)} %fusion.44, bf16[8,128,128]{1,2,0:T(8,128)(2,1)S(1)} %fusion.40, bf16[1024,1024]{1,0:T(8,128)(2,1)S(1)} %copy-done), kind=kOutput, calls=%fused_computation.12 | convolution fusion | flops 270532608 | bytes 8650752 | tf_op jit(solution)/shard_map/shb,hab->sha/dot_general | solution.py:91
  241.3 3.9 %copy.56 = bf16[1024,1024]{1,0:T(8,128)(2,1)} copy(bf16[1024,1024]{0,1:T(8,128)(2,1)} %bitcast.131) | data formatting | bytes 4194304
  (45 shorter events, 0.6 us)
Async XLA Ops:
  0.6 7.8 %copy-start = (bf16[1024,1024]{1,0:T(8,128)(2,1)S(1)}, bf16[1024,1024]{1,0:T(8,128)(2,1)}, u32[]{:S(2)}) copy-start(bf16[1024,1024]{1,0:T(8,128)(2,1)} %param.8) | copy-start | bytes 6291460
  10.8 10.7 %copy-start.5 = (f32[8,128,128]{2,1,0:T(8,128)}, f32[8,128,128]{2,1,0:T(8,128)S(1)}, u32[]{:S(2)}) copy-start(f32[8,128,128]{2,1,0:T(8,128)S(1)} %fusion.15) | copy-start | bytes 1572868
  10.8 15.1 %collective-permute-start = (f32[8,128,128]{2,1,0:T(8,128)S(1)}, f32[8,128,128]{2,1,0:T(8,128)}, u32[]{:S(2)}, u32[]{:S(2)}) collective-permute-start(f32[8,128,128]{2,1,0:T(8,128)S(1)} %fusion.15), channel_id=1, source_target_pairs={{0,4},{4,0},{8,12},{12,8},{16,20},{20,16},{24,28},{28,24},{1,5},{5... | collective-permute-start | bytes 1572872 | tf_op jit(solution)/shard_map/ppermute | solution.py:18
  21.8 7.2 %copy-start.3 = (pred[1024,1024]{1,0:T(8,128)(4,1)}, pred[1024,1024]{1,0:T(8,128)(4,1)S(1)}, u32[]{:S(2)}) copy-start(pred[1024,1024]{1,0:T(8,128)(4,1)S(1)} %iota_compare_fusion) | copy-start | bytes 3145732
  27.2 17.7 %copy-start.6 = (f32[4,8,1024]{2,1,0:T(8,128)S(1)}, f32[4,8,1024]{2,1,0:T(8,128)}, u32[]{:S(2)}) copy-start(f32[4,8,1024]{2,1,0:T(8,128)} %param.9) | copy-start | bytes 393220
  27.2 13.3 %collective-permute-start.1 = (f32[8,128,128]{2,1,0:T(8,128)S(1)}, f32[8,128,128]{2,1,0:T(8,128)}, u32[]{:S(2)}, u32[]{:S(2)}) collective-permute-start(f32[8,128,128]{2,1,0:T(8,128)S(1)} %get-tuple-element.28), channel_id=1, source_target_pairs={{0,8},{8,0},{4,12},{12,4},{16,24},{24,16},{20,28},{28,20},{1,9},{9... | collective-permute-start | bytes 1572872 | tf_op jit(solution)/shard_map/ppermute | solution.py:18
  42.4 24.7 %collective-permute-start.2 = (f32[8,128,128]{2,1,0:T(8,128)}, f32[8,128,128]{2,1,0:T(8,128)}, u32[]{:S(2)}, u32[]{:S(2)}) collective-permute-start(f32[8,128,128]{2,1,0:T(8,128)} %get-tuple-element.30), channel_id=1, source_target_pairs={{0,16},{16,0},{4,20},{20,4},{8,24},{24,8},{12,28},{28,12},{1,17},{... | collective-permute-start | bytes 1572872 | tf_op jit(solution)/shard_map/ppermute | solution.py:18
  78.5 17.7 %copy-start.7 = (f32[1024]{0:T(1024)S(1)}, f32[1024]{0:T(1024)}, u32[]{:S(2)}) copy-start(f32[1024]{0:T(1024)} %param.10) | copy-start | bytes 12292
  108.5 7.2 %slice-start = ((s8[12582912]{0:T(1024)(128)(4,1)}), s8[4194304]{0:T(1024)(128)(4,1)S(1)}, s32[]{:S(2)}) async-start(s8[12582912]{0:T(1024)(128)(4,1)} %bitcast.117), calls=%async_computation | async-start | bytes 8388608
  108.5 8.2 %slice-start.1 = ((s8[12582912]{0:T(1024)(128)(4,1)}), s8[4194304]{0:T(1024)(128)(4,1)S(1)}, s32[]{:S(2)}) async-start(s8[12582912]{0:T(1024)(128)(4,1)} %bitcast.117), calls=%async_computation.1 | async-start | bytes 8388608
  108.5 9.8 %slice-start.2 = ((s8[12582912]{0:T(1024)(128)(4,1)}), s8[4194304]{0:T(1024)(128)(4,1)S(1)}, s32[]{:S(2)}) async-start(s8[12582912]{0:T(1024)(128)(4,1)} %bitcast.117), calls=%async_computation.2 | async-start | bytes 8388608
  115.2 12.4 %copy-start.2 = (bf16[1024,8,128]{0,2,1:T(8,128)(2,1)}, bf16[1024,8,128]{0,2,1:T(8,128)(2,1)S(1)}, u32[]{:S(2)}) copy-start(bf16[1024,8,128]{0,2,1:T(8,128)(2,1)S(1)} %get-tuple-element.21) | copy-start | bytes 6291460
  118.3 5.1 %copy-start.1 = (bf16[128,8,8,128]{3,2,1,0:T(8,128)(2,1)S(1)}, bf16[128,8,8,128]{3,2,1,0:T(8,128)(2,1)}, u32[]{:S(2)}) copy-start(bf16[128,8,8,128]{3,2,1,0:T(8,128)(2,1)} %copy.74) | copy-start | bytes 6291460
  123.4 4.2 %copy-start.4 = (pred[1024,1024]{1,0:T(8,128)(4,1)S(1)}, pred[1024,1024]{1,0:T(8,128)(4,1)}, u32[]{:S(2)}) copy-start(pred[1024,1024]{1,0:T(8,128)(4,1)} %copy-done.3) | copy-start | bytes 3145732
  126.4 35.6 %collective-permute-start.3 = (f32[3,8,128,128]{2,3,0,1:T(8,128)}, f32[3,8,128,128]{2,3,0,1:T(8,128)}, u32[]{:S(2)}, u32[]{:S(2)}) collective-permute-start(f32[3,8,128,128]{2,3,0,1:T(8,128)} %multiply_bitcast_fusion), channel_id=1, source_target_pairs={{0,4},{4,0},{8,12},{12,8},{16,20},{20,16},{24,28},{28,24},{1,5},{5... | collective-permute-start | bytes 4718600 | tf_op jit(solution)/shard_map/ppermute | solution.py:18
  137.3 29.0 %slice-start.3 = ((s8[16777216]{0:T(1024)(128)(4,1)}), s8[4194304]{0:T(1024)(128)(4,1)S(1)}, s32[]{:S(2)}) async-start(s8[16777216]{0:T(1024)(128)(4,1)} %bitcast.119), calls=%async_computation.3 | async-start | bytes 8388608
  137.3 29.0 %slice-start.4 = ((s8[16777216]{0:T(1024)(128)(4,1)}), s8[4194304]{0:T(1024)(128)(4,1)S(1)}, s32[]{:S(2)}) async-start(s8[16777216]{0:T(1024)(128)(4,1)} %bitcast.119), calls=%async_computation.4 | async-start | bytes 8388608
  137.3 29.0 %slice-start.5 = ((s8[16777216]{0:T(1024)(128)(4,1)}), s8[4194304]{0:T(1024)(128)(4,1)S(1)}, s32[]{:S(2)}) async-start(s8[16777216]{0:T(1024)(128)(4,1)} %bitcast.119), calls=%async_computation.5 | async-start | bytes 8388608
  148.7 17.6 %slice-start.6 = ((s8[16777216]{0:T(1024)(128)(4,1)}), s8[4194304]{0:T(1024)(128)(4,1)S(1)}, s32[]{:S(2)}) async-start(s8[16777216]{0:T(1024)(128)(4,1)} %bitcast.119), calls=%async_computation.6 | async-start | bytes 8388608
  162.0 31.4 %slice-start.7 = ((s8[6291456]{0:T(1024)(128)(4,1)}), s8[4194304]{0:T(1024)(128)(4,1)S(1)}, s32[]{:S(2)}) async-start(s8[6291456]{0:T(1024)(128)(4,1)} %bitcast.125), calls=%async_computation.7 | async-start | bytes 8388608
  164.8 28.6 %slice-start.8 = ((s8[6291456]{0:T(1024)(128)(4,1)}), s8[2097152]{0:T(1024)(128)(4,1)S(1)}, s32[]{:S(2)}) async-start(s8[6291456]{0:T(1024)(128)(4,1)} %bitcast.125), calls=%async_computation.8 | async-start | bytes 4194304
  164.8 23.9 %collective-permute-start.4 = (f32[2,8,128,128]{2,3,0,1:T(8,128)}, f32[2,8,128,128]{2,3,0,1:T(8,128)}, u32[]{:S(2)}, u32[]{:S(2)}) collective-permute-start(f32[2,8,128,128]{2,3,0,1:T(8,128)} %slice_add_fusion), channel_id=1, source_target_pairs={{0,8},{8,0},{4,12},{12,4},{16,24},{24,16},{20,28},{28,20},{1,9},{9... | collective-permute-start | bytes 3145736 | tf_op jit(solution)/shard_map/ppermute | solution.py:18
  190.0 36.7 %collective-permute-start.5 = (f32[1,8,128,128]{2,3,0,1:T(8,128)S(1)}, f32[1,8,128,128]{2,3,0,1:T(8,128)}, u32[]{:S(2)}, u32[]{:S(2)}) collective-permute-start(f32[1,8,128,128]{2,3,0,1:T(8,128)S(1)} %slice_add_fusion.1), channel_id=1, source_target_pairs={{0,16},{16,0},{4,20},{20,4},{8,24},{24,8},{12,28},{28,12},{1,17},{... | collective-permute-start | bytes 1572872 | tf_op jit(solution)/shard_map/ppermute | solution.py:18
where the time goes:
time: 246 us; the launch traced here: 245 us
  matrix products  90.1 us (37%)
  waiting for transfers between devices  41.6 us (17%)
  local copies, waits for them, and re-layouts  38.8 us (16%)
  blocking collectives  32.7 us (13%)
  other arithmetic  27.4 us (11%)
  starting transfers between devices  13.7 us (6%)
    ppermute x6, waiting for transfers between devices, from_partner(): return lax.ppermute(block, axis, route)  41.6 us
    unnamed x41, local copies, waits for them, and re-layouts  26.4 us
    psum x1, blocking collectives, body(): grad_gain = lax.psum(jnp.sum(cot_three * normed, axis=0).reshape(-1), 'seq')  20.6 us
    ppermute x6, starting transfers between devices, from_partner(): return lax.ppermute(block, axis, route)  13.7 us
    dot_general x1, matrix products, body(): jnp.einsum('hts,she->the', kept, v_three, preferred_element_type=f32)  12.1 us
    dot_general x1, matrix products, body(): jnp.einsum('hts,she->the', pair, k_three, preferred_element_type=f32)  11.4 us
    dot_general x1, matrix products, body(): jnp.einsum('hts,the->she', kept, weighted, preferred_element_type=f32)  10.9 us
    dot_general x1, matrix products, body(): jnp.einsum('the,she->hts', q_three, k_three, preferred_element_type=f32)  10.4 us
  transfers between devices with their start and end apart: 6, of which 5 were waited for; matrix products, arithmetic and copies ran while one was open for 30% of the time, Pallas kernels for 0%

commit v1 on v0

--- a/solution.py
+++ b/solution.py
@@ -55,7 +55,9 @@
     gain_three = gain.reshape(heads_here, width)
     mixed = (normed * gain_three).astype(bf16).reshape(rows, -1)
     cot_three = cotangent.reshape(rows, heads_here, width).astype(f32)
-    grad_gain = lax.psum(jnp.sum(cot_three * normed, axis=0).reshape(-1), "seq")
+    block_2 = jnp.sum(cot_three * normed, axis=0).reshape(-1)
+    parts = lax.all_gather(block_2, "seq")
+    grad_gain = jnp.sum(parts, axis=0)
     weighted_cot = cot_three * gain_three
     inner = lax.psum(jnp.sum(weighted_cot * output, axis=(1, 2)), "head")
     grad_full = (

time: 246 us -> 257 us (1.045)
  blocking collectives: 32.7 us -> 43.3 us
    all_gather x0 -> x1, blocking collectives: none -> 31.2 us  [body(): parts = lax.all_gather(block_2, 'seq')]
    psum x1 -> x0, blocking collectives: 20.6 us -> none  [body(): grad_gain = lax.psum(jnp.sum(cot_three * normed, axis=0).reshape(-1), 'seq')]
    reduce_sum x1 -> x2, other arithmetic: 5.73 us -> 6.35 us  [the longest x1 5.73 us: body(): block_2 = jnp.sum(cot_three * normed, axis=0).reshape(-1)]
  transfers between devices with their start and end apart: 6 -> 6, of which waited for: 5 -> 5; matrix products, arithmetic and copies ran while one was open for 30% -> 29% of each run, Pallas kernels for 0% -> 0%
where the time goes in v1:
time: 257 us; the launch traced here: 256 us
  matrix products  90.1 us (35%)
  blocking collectives  43.3 us (17%)
  waiting for transfers between devices  41.6 us (16%)
  local copies, waits for them, and re-layouts  38.8 us (15%)
  other arithmetic  28 us (11%)
  starting transfers between devices  13.7 us (5%)
    ppermute x6, waiting for transfers between devices, from_partner(): return lax.ppermute(block, axis, route)  41.6 us
    all_gather x1, blocking collectives, body(): parts = lax.all_gather(block_2, 'seq')  31.2 us
    unnamed x41, local copies, waits for them, and re-layouts  26.4 us
    ppermute x6, starting transfers between devices, from_partner(): return lax.ppermute(block, axis, route)  13.7 us
    dot_general x1, matrix products, body(): jnp.einsum('hts,she->the', kept, v_three, preferred_element_type=f32)  12.1 us
    dot_general x1, matrix products, body(): jnp.einsum('hts,she->the', pair, k_three, preferred_element_type=f32)  11.4 us
    dot_general x1, matrix products, body(): jnp.einsum('hts,the->she', kept, weighted, preferred_element_type=f32)  10.9 us
    dot_general x1, matrix products, body(): jnp.einsum('the,she->hts', q_three, k_three, preferred_element_type=f32)  10.4 us
  transfers between devices with their start and end apart: 6, of which 5 were waited for; matrix products, arithmetic and copies ran while one was open for 29% of the time, Pallas kernels for 0%

profile of v1, /device:TPU:0, one launch (start us, length us, event | category | flops | bytes accessed | tf_op | source)
XLA Modules:
  0.0 256.5 jit_solution(8038491470330482446)
XLA Ops:
  0.6 3.7 %copy.75 = bf16[128,8,8,128]{3,2,1,0:T(8,128)(2,1)} copy(bf16[128,8,8,128]{3,1,2,0:T(8,128)(2,1)} %bitcast.130) | data formatting | bytes 4194304
  4.3 4.1 %copy.39 = bf16[1024,8,128]{0,2,1:T(8,128)(2,1)} copy(bf16[1024,8,128]{2,1,0:T(8,128)(2,1)} %bitcast.129) | data formatting | bytes 4194304 | tf_op jit(solution)/shard_map/reshape | solution.py:30
  8.4 2.3 fusion.15
  10.8 3.1 %collective-permute-start = (f32[8,128,128]{2,1,0:T(8,128)S(1)}, f32[8,128,128]{2,1,0:T(8,128)}, u32[]{:S(2)}, u32[]{:S(2)}) collective-permute-start(f32[8,128,128]{2,1,0:T(8,128)S(1)} %fusion.15), channel_id=1, source_target_pairs={{0,4},{4,0},{8,12},{12,8},{16,20},{20,16},{24,28},{28,24},{1,5},{5... | collective-permute-start | bytes 1572872 | tf_op jit(solution)/shard_map/ppermute | solution.py:18
  13.9 3.5 %copy.74 = bf16[128,8,8,128]{3,2,1,0:T(8,128)(2,1)} copy(bf16[128,8,8,128]{3,1,2,0:T(8,128)(2,1)} %bitcast.133) | data formatting | bytes 4194304
  17.4 4.1 %copy.49 = bf16[1024,8,128]{0,2,1:T(8,128)(2,1)} copy(bf16[1024,8,128]{2,1,0:T(8,128)(2,1)} %bitcast.122) | data formatting | bytes 4194304 | tf_op jit(solution)/shard_map/reshape | solution.py:29
  21.8 4.1 %collective-permute-done = f32[8,128,128]{2,1,0:T(8,128)} collective-permute-done((f32[8,128,128]{2,1,0:T(8,128)S(1)}, f32[8,128,128]{2,1,0:T(8,128)}, u32[]{:S(2)}, u32[]{:S(2)}) %collective-permute-start) | collective-permute-done | bytes 524320 | tf_op jit(solution)/shard_map/ppermute | solution.py:18
  25.9 1.3 fusion.37
  27.2 1.9 collective-permute-start.1
  29.1 10.4 %select_convert_fusion.1 = bf16[8,1024,1024]{2,1,0:T(8,128)(2,1)} fusion(pred[1024,1024]{1,0:T(8,128)(4,1)S(1)} %iota_compare_fusion, bf16[1024,8,128]{0,2,1:T(8,128)(2,1)} %copy.49, bf16[1024,1024]{1,0:T(8,128)(2,1)} %param.7), kind=kOutput, calls=%fused_computation.1 | convolution fusion | flops 2164260864 | bytes 22020096 | tf_op jit(solution)/shard_map/the,she->hts/dot_general | solution.py:32
  39.4 1.0 collective-permute-done.1
  40.4 1.9 fusion.38
  42.4 2.5 collective-permute-start.2
  45.0 4.1 %copy.43 = f32[1024,1024]{0,1:T(8,128)} copy(bf16[1024,1024]{1,0:T(8,128)(2,1)} %param.11) | data formatting | bytes 6291456 | tf_op jit(solution)/shard_map/convert_element_type | solution.py:57
  49.2 17.9 %collective-permute-done.2 = f32[8,128,128]{2,1,0:T(8,128)} collective-permute-done((f32[8,128,128]{2,1,0:T(8,128)}, f32[8,128,128]{2,1,0:T(8,128)}, u32[]{:S(2)}, u32[]{:S(2)}) %collective-permute-start.2) | collective-permute-done | bytes 524320 | tf_op jit(solution)/shard_map/ppermute | solution.py:18
  67.0 1.1 fusion.39
  68.1 10.4 %fusion = (f32[1024,8,128]{0,2,1:T(8,128)}, f32[8,3,128,1024]{3,2,1,0:T(8,128)}) fusion(f32[3,1024,8]{1,0,2:T(4,128)S(1)} %copy.38, bf16[1024,8,128,1]{2,1,0,3:T(8,128)(2,1)} %bitcast.123, bf16[1,8,128,128]{3,2,1,0:T(8,128)(2,1)S(1)} %fusion.39, bf16[1,8,128,128]{3,2,1,0:T(8,128)(2,1)S(1)} %get-tuple-element.29, ...), kind=kOutput, calls=%fused_computation.4 | convolution fusion | flops 811335680 | bytes 19759104 | tf_op jit(solution)/shard_map/the,lhef->lthf/dot_general | solution.py:48
  78.5 12.1 %multiply_reduce_fusion.2 = (f32[1024]{0:T(1024)S(1)}, f32[1024,8,128]{0,2,1:T(8,128)}, f32[8,1024,128]{1,2,0:T(8,128)}) fusion(f32[1024,8,128]{0,2,1:T(8,128)} %get-tuple-element.33, f32[1024,8]{0,1:T(8,128)S(1)} %get-tuple-element.32, bf16[8,1024,1024]{2,1,0:T(8,128)(2,1)} %select_convert_fusion.1, bf16[1024,1024]{1,0:T(8,128)(2,1)S(1)} %copy-done), kind=kOutput, calls=%fused_computation.23 | convolution fusion | flops 2151676928 | bytes 31494144 | tf_op jit(solution)/shard_map/hts,she->the/dot_general | solution.py:37
  90.6 5.6 %psum.14 = f32[1024]{0:T(1024)S(1)} all-reduce(f32[1024]{0:T(1024)S(1)} %get-tuple-element.22), channel_id=1, replica_groups=mesh['seq'=8,'head'=4] {'head'}, use_global_device_ids=true, to_apply=%region_2.3 | all-reduce | flops 1024 | bytes 8192 | tf_op jit(solution)/shard_map/psum | solution.py:52
  96.2 5.7 %multiply_reduce_fusion = (f32[8,128]{1,0:T(8,128)S(1)}, f32[1024]{0:T(1024)S(1)}) fusion(f32[1024,8,128]{0,2,1:T(8,128)} %bitcast.121, f32[1024,8,128]{0,2,1:T(8,128)} %get-tuple-element.23, f32[1024]{0:T(1024)S(1)} %add_rsqrt_fusion, f32[8,128]{1,0:T(8,128)S(1)} %bitcast.136, f32[1024,1024]{0,1:T(8,128)} %copy.43), kind=kLoop, calls=%fused_computation.17 | loop fusion | flops 6289408 | bytes 12599296 | tf_op jit(solution)/shard_map/reduce_sum | solution.py:58
  101.9 6.5 %psum.15 = f32[1024]{0:T(1024)S(1)} all-reduce(f32[1024]{0:T(1024)S(1)} %get-tuple-element.19), channel_id=1, replica_groups=mesh['seq'=8,'head'=4] {'head'}, use_global_device_ids=true, to_apply=%region_4.5 | all-reduce | flops 1024 | bytes 8192 | tf_op jit(solution)/shard_map/psum | solution.py:62
  108.5 6.7 %fusion.7 = (f32[1024,8]{0,1:T(8,128)S(1)}, bf16[1024,8,128]{0,2,1:T(8,128)(2,1)S(1)}, bf16[1024,8,128]{0,2,1:T(8,128)(2,1)}) fusion(f32[8,1024,128]{1,2,0:T(8,128)} %get-tuple-element.35, f32[1024]{0:T(1024)S(1)} %add_rsqrt_fusion, f32[1024,8,128]{0,2,1:T(8,128)} %get-tuple-element.23, f32[1024]{0:T(1024)S(1)} %fusion.41, f32[8,128]{1,0:T(8,128)S(1)} %bitcast.137, ...), kind=kLoop, calls=%fused_computation.16 | loop fusion | flops 11526144 | bytes 16822272 | tf_op jit(solution)/shard_map/reduce_sum | solution.py:68
  115.7 1.0 slice-done.1
  116.7 1.6 slice-done.2
  118.3 4.3 %fusion.1 = (f32[3,1024,8]{1,0,2:T(4,128)S(1)}, bf16[3,1024,8,128]{1,3,0,2:T(8,128)(2,1)}) fusion(f32[8,3,128,1024]{3,2,1,0:T(8,128)S(1)} %bitcast.118, f32[1024,8,128]{0,2,1:T(8,128)S(1)} %convert_element_type.64, f32[3,1024,8]{1,0,2:T(4,128)S(1)} %copy.38), kind=kLoop, calls=%fused_computation.5 | loop fusion | flops 12558336 | bytes 23265280 | tf_op jit(solution)/shard_map/reduce_sum | solution.py:69
  122.7 0.7 copy.58
  123.4 3.0 %multiply_bitcast_fusion = f32[3,8,128,128]{2,3,0,1:T(8,128)} fusion(bf16[1024,8,128,1]{2,1,0,3:T(8,128)(2,1)S(1)} %bitcast.124, f32[3]{0:T(128)S(1)} %pad_maximum_fusion.2, f32[1024,8,128]{0,2,1:T(8,128)S(1)} %convert_element_type.64, f32[3,1024,8]{1,0,2:T(4,128)S(1)} %copy.38), kind=kOutput, calls=%fused_computation.42 | convolution fusion | flops 811991040 | bytes 7962636 | tf_op jit(solution)/shard_map/the,lthf->lhef/dot_general | solution.py:84
  126.4 1.3 collective-permute-start.3
  127.6 9.6 %select_convert_fusion = bf16[8,1024,1024]{2,1,0:T(8,128)(2,1)} fusion(f32[8,1024]{1,0:T(8,128)S(1)} %get-tuple-element.31, pred[1024,1024]{1,0:T(8,128)(4,1)S(1)} %copy-done.4, bf16[1024,8,128]{0,2,1:T(8,128)(2,1)S(1)} %get-tuple-element.21, bf16[1024,1024]{1,0:T(8,128)(2,1)S(1)} %copy-done), kind=kOutput, calls=%fused_computation | convolution fusion | flops 2172649472 | bytes 22052864 | tf_op jit(solution)/shard_map/the,she->hts/dot_general | solution.py:74
  137.3 11.4 %fusion.43 = f32[8,1024,128]{1,2,0:T(8,128)} fusion(bf16[8,1024,1024]{2,1,0:T(8,128)(2,1)} %select_convert_fusion, bf16[1024,8,128]{0,2,1:T(8,128)(2,1)} %copy.39), kind=kOutput, calls=%fused_computation.71 | convolution fusion | flops 2147483648 | bytes 23068672 | tf_op jit(solution)/shard_map/hts,she->the/dot_general | solution.py:78
  148.7 10.9 %fusion.10 = f32[8,128,1024]{2,1,0:T(8,128)} fusion(bf16[8,1024,1024]{2,1,0:T(8,128)(2,1)} %select_convert_fusion.1, bf16[1024,8,128]{0,2,1:T(8,128)(2,1)} %copy-done.2, f32[1024,8]{0,1:T(8,128)S(1)} %get-tuple-element.32), kind=kOutput, calls=%fused_computation.25 | convolution fusion | flops 2150629376 | bytes 23101440 | tf_op jit(solution)/shard_map/hts,the->she/dot_general | solution.py:72
  159.6 2.4 collective-permute-done.3
  162.0 2.8 %slice_add_fusion = f32[2,8,128,128]{2,3,0,1:T(8,128)} fusion(f32[3,8,128,128]{2,3,0,1:T(8,128)} %collective-permute-done.3, f32[3,8,128,128]{2,3,0,1:T(8,128)} %multiply_bitcast_fusion), kind=kLoop, calls=%fused_computation.47 | loop fusion | flops 262144 | bytes 3145728 | tf_op jit(solution)/shard_map/add | solution.py:91
  164.8 1.5 collective-permute-start.4
  166.3 6.1 %fusion.44 = f32[8,1024,128]{1,2,0:T(8,128)} fusion(bf16[1024,8,128]{0,2,1:T(8,128)(2,1)} %copy.49, bf16[8,1024,1024]{2,1,0:T(8,128)(2,1)S(1)} %bitcast.120), kind=kOutput, calls=%fused_computation.72 | convolution fusion | flops 2147483648 | bytes 23068672 | tf_op jit(solution)/shard_map/hts,the->she/dot_general | solution.py:79
  172.4 16.3 %collective-permute-done.4 = f32[2,8,128,128]{2,3,0,1:T(8,128)} collective-permute-done((f32[2,8,128,128]{2,3,0,1:T(8,128)}, f32[2,8,128,128]{2,3,0,1:T(8,128)}, u32[]{:S(2)}, u32[]{:S(2)}) %collective-permute-start.4) | collective-permute-done | bytes 1048608 | tf_op jit(solution)/shard_map/ppermute | solution.py:18
  188.7 1.3 slice_add_fusion.1
  190.0 3.4 %collective-permute-start.5 = (f32[1,8,128,128]{2,3,0,1:T(8,128)S(1)}, f32[1,8,128,128]{2,3,0,1:T(8,128)}, u32[]{:S(2)}, u32[]{:S(2)}) collective-permute-start(f32[1,8,128,128]{2,3,0,1:T(8,128)S(1)} %slice_add_fusion.1), channel_id=1, source_target_pairs={{0,16},{16,0},{4,20},{20,4},{8,24},{24,8},{12,28},{28,12},{1,17},{... | collective-permute-start | bytes 1572872 | tf_op jit(solution)/shard_map/ppermute | solution.py:18
  193.4 4.8 %fusion.4 = bf16[1024,8,128]{0,2,1:T(8,128)(2,1)} fusion(f32[8,1024,128]{1,2,0:T(8,128)} %fusion.43, bf16[3,1024,8,128]{1,3,0,2:T(8,128)(2,1)S(1)} %bitcast.126, bf16[1,8,128,128]{3,2,1,0:T(8,128)(2,1)S(1)} %fusion.39, bf16[1,8,128,128]{3,2,1,0:T(8,128)(2,1)S(1)} %get-tuple-element.29, bf16[1,8,128,128]{3,2,1,0:T(8,128)(2,1)S(1)} %get-tuple-element.27), kind=kOutput, calls=%fused_computation.10 | convolution fusion | flops 808189952 | bytes 13369344 | tf_op jit(solution)/shard_map/lthf,lhef->the/dot_general | solution.py:81
  198.2 3.9 %copy.55 = bf16[1024,1024]{1,0:T(8,128)(2,1)} copy(bf16[1024,1024]{0,1:T(8,128)(2,1)} %bitcast.128) | data formatting | bytes 4194304
  202.1 3.9 %copy.54 = bf16[1024,1024]{1,0:T(8,128)(2,1)} copy(bf16[1024,1024]{0,1:T(8,128)(2,1)} %bitcast.127) | data formatting | bytes 4194304
  206.0 31.2 %all-gather = f32[8,1,1024]{2,1,0:T(1,128)S(1)} all-gather(f32[1,1,1024]{2,1,0:T(1,128)S(1)} %bitcast.138), channel_id=1, replica_groups=mesh['seq'=8,'head'=4] {'seq'}, dimensions={0}, use_global_device_ids=true | all-gather | bytes 36864 | tf_op jit(solution)/shard_map/all_gather | solution.py:59
  237.2 0.6 reduce_sum.69
  237.8 1.5 fusion.40
  239.3 4.9 %add_convert_fusion = bf16[8,128,1024]{2,1,0:T(8,128)(2,1)} fusion(f32[8,128,1024]{2,1,0:T(8,128)} %fusion.10, bf16[8,128,128]{1,2,0:T(8,128)(2,1)S(1)} %fusion.40, bf16[1024,1024]{1,0:T(8,128)(2,1)} %param.7), kind=kOutput, calls=%fused_computation.18 | convolution fusion | flops 270532608 | bytes 8650752 | tf_op jit(solution)/shard_map/sha,hab->shb/dot_general | solution.py:94
  244.2 3.9 %copy.57 = bf16[1024,1024]{1,0:T(8,128)(2,1)} copy(bf16[1024,1024]{0,1:T(8,128)(2,1)} %bitcast.132) | data formatting | bytes 4194304
  248.2 4.3 %fusion.5 = bf16[1024,8,128]{0,2,1:T(8,128)(2,1)} fusion(f32[8,1024,128]{1,2,0:T(8,128)} %fusion.44, bf16[8,128,128]{1,2,0:T(8,128)(2,1)S(1)} %fusion.40, bf16[1024,1024]{1,0:T(8,128)(2,1)S(1)} %copy-done), kind=kOutput, calls=%fused_computation.12 | convolution fusion | flops 270532608 | bytes 8650752 | tf_op jit(solution)/shard_map/shb,hab->sha/dot_general | solution.py:93
  252.5 3.9 %copy.56 = bf16[1024,1024]{1,0:T(8,128)(2,1)} copy(bf16[1024,1024]{0,1:T(8,128)(2,1)} %bitcast.131) | data formatting | bytes 4194304
  (46 shorter events, 1.1 us)
Async XLA Ops:
  0.6 7.8 %copy-start = (bf16[1024,1024]{1,0:T(8,128)(2,1)S(1)}, bf16[1024,1024]{1,0:T(8,128)(2,1)}, u32[]{:S(2)}) copy-start(bf16[1024,1024]{1,0:T(8,128)(2,1)} %param.8) | copy-start | bytes 6291460
  10.8 10.7 %copy-start.5 = (f32[8,128,128]{2,1,0:T(8,128)}, f32[8,128,128]{2,1,0:T(8,128)S(1)}, u32[]{:S(2)}) copy-start(f32[8,128,128]{2,1,0:T(8,128)S(1)} %fusion.15) | copy-start | bytes 1572868
  10.8 15.1 %collective-permute-start = (f32[8,128,128]{2,1,0:T(8,128)S(1)}, f32[8,128,128]{2,1,0:T(8,128)}, u32[]{:S(2)}, u32[]{:S(2)}) collective-permute-start(f32[8,128,128]{2,1,0:T(8,128)S(1)} %fusion.15), channel_id=1, source_target_pairs={{0,4},{4,0},{8,12},{12,8},{16,20},{20,16},{24,28},{28,24},{1,5},{5... | collective-permute-start | bytes 1572872 | tf_op jit(solution)/shard_map/ppermute | solution.py:18
  21.8 7.2 %copy-start.3 = (pred[1024,1024]{1,0:T(8,128)(4,1)}, pred[1024,1024]{1,0:T(8,128)(4,1)S(1)}, u32[]{:S(2)}) copy-start(pred[1024,1024]{1,0:T(8,128)(4,1)S(1)} %iota_compare_fusion) | copy-start | bytes 3145732
  27.2 17.7 %copy-start.6 = (f32[4,8,1024]{2,1,0:T(8,128)S(1)}, f32[4,8,1024]{2,1,0:T(8,128)}, u32[]{:S(2)}) copy-start(f32[4,8,1024]{2,1,0:T(8,128)} %param.9) | copy-start | bytes 393220
  27.2 13.3 %collective-permute-start.1 = (f32[8,128,128]{2,1,0:T(8,128)S(1)}, f32[8,128,128]{2,1,0:T(8,128)}, u32[]{:S(2)}, u32[]{:S(2)}) collective-permute-start(f32[8,128,128]{2,1,0:T(8,128)S(1)} %get-tuple-element.28), channel_id=1, source_target_pairs={{0,8},{8,0},{4,12},{12,4},{16,24},{24,16},{20,28},{28,20},{1,9},{9... | collective-permute-start | bytes 1572872 | tf_op jit(solution)/shard_map/ppermute | solution.py:18
  42.4 24.7 %collective-permute-start.2 = (f32[8,128,128]{2,1,0:T(8,128)}, f32[8,128,128]{2,1,0:T(8,128)}, u32[]{:S(2)}, u32[]{:S(2)}) collective-permute-start(f32[8,128,128]{2,1,0:T(8,128)} %get-tuple-element.30), channel_id=1, source_target_pairs={{0,16},{16,0},{4,20},{20,4},{8,24},{24,8},{12,28},{28,12},{1,17},{... | collective-permute-start | bytes 1572872 | tf_op jit(solution)/shard_map/ppermute | solution.py:18
  78.5 17.7 %copy-start.7 = (f32[1024]{0:T(1024)S(1)}, f32[1024]{0:T(1024)}, u32[]{:S(2)}) copy-start(f32[1024]{0:T(1024)} %param.10) | copy-start | bytes 12292
  108.5 7.2 %slice-start = ((s8[12582912]{0:T(1024)(128)(4,1)}), s8[4194304]{0:T(1024)(128)(4,1)S(1)}, s32[]{:S(2)}) async-start(s8[12582912]{0:T(1024)(128)(4,1)} %bitcast.117), calls=%async_computation | async-start | bytes 8388608
  108.5 8.2 %slice-start.1 = ((s8[12582912]{0:T(1024)(128)(4,1)}), s8[4194304]{0:T(1024)(128)(4,1)S(1)}, s32[]{:S(2)}) async-start(s8[12582912]{0:T(1024)(128)(4,1)} %bitcast.117), calls=%async_computation.1 | async-start | bytes 8388608
  108.5 9.8 %slice-start.2 = ((s8[12582912]{0:T(1024)(128)(4,1)}), s8[4194304]{0:T(1024)(128)(4,1)S(1)}, s32[]{:S(2)}) async-start(s8[12582912]{0:T(1024)(128)(4,1)} %bitcast.117), calls=%async_computation.2 | async-start | bytes 8388608
  115.2 12.4 %copy-start.2 = (bf16[1024,8,128]{0,2,1:T(8,128)(2,1)}, bf16[1024,8,128]{0,2,1:T(8,128)(2,1)S(1)}, u32[]{:S(2)}) copy-start(bf16[1024,8,128]{0,2,1:T(8,128)(2,1)S(1)} %get-tuple-element.21) | copy-start | bytes 6291460
  118.3 5.1 %copy-start.1 = (bf16[128,8,8,128]{3,2,1,0:T(8,128)(2,1)S(1)}, bf16[128,8,8,128]{3,2,1,0:T(8,128)(2,1)}, u32[]{:S(2)}) copy-start(bf16[128,8,8,128]{3,2,1,0:T(8,128)(2,1)} %copy.74) | copy-start | bytes 6291460
  123.4 4.2 %copy-start.4 = (pred[1024,1024]{1,0:T(8,128)(4,1)S(1)}, pred[1024,1024]{1,0:T(8,128)(4,1)}, u32[]{:S(2)}) copy-start(pred[1024,1024]{1,0:T(8,128)(4,1)} %copy-done.3) | copy-start | bytes 3145732
  126.4 35.6 %collective-permute-start.3 = (f32[3,8,128,128]{2,3,0,1:T(8,128)}, f32[3,8,128,128]{2,3,0,1:T(8,128)}, u32[]{:S(2)}, u32[]{:S(2)}) collective-permute-start(f32[3,8,128,128]{2,3,0,1:T(8,128)} %multiply_bitcast_fusion), channel_id=1, source_target_pairs={{0,4},{4,0},{8,12},{12,8},{16,20},{20,16},{24,28},{28,24},{1,5},{5... | collective-permute-start | bytes 4718600 | tf_op jit(solution)/shard_map/ppermute | solution.py:18
  137.3 29.0 %slice-start.3 = ((s8[16777216]{0:T(1024)(128)(4,1)}), s8[4194304]{0:T(1024)(128)(4,1)S(1)}, s32[]{:S(2)}) async-start(s8[16777216]{0:T(1024)(128)(4,1)} %bitcast.119), calls=%async_computation.3 | async-start | bytes 8388608
  137.3 29.0 %slice-start.4 = ((s8[16777216]{0:T(1024)(128)(4,1)}), s8[4194304]{0:T(1024)(128)(4,1)S(1)}, s32[]{:S(2)}) async-start(s8[16777216]{0:T(1024)(128)(4,1)} %bitcast.119), calls=%async_computation.4 | async-start | bytes 8388608
  137.3 29.0 %slice-start.5 = ((s8[16777216]{0:T(1024)(128)(4,1)}), s8[4194304]{0:T(1024)(128)(4,1)S(1)}, s32[]{:S(2)}) async-start(s8[16777216]{0:T(1024)(128)(4,1)} %bitcast.119), calls=%async_computation.5 | async-start | bytes 8388608
  148.7 17.6 %slice-start.6 = ((s8[16777216]{0:T(1024)(128)(4,1)}), s8[4194304]{0:T(1024)(128)(4,1)S(1)}, s32[]{:S(2)}) async-start(s8[16777216]{0:T(1024)(128)(4,1)} %bitcast.119), calls=%async_computation.6 | async-start | bytes 8388608
  162.0 31.4 %slice-start.7 = ((s8[6291456]{0:T(1024)(128)(4,1)}), s8[4194304]{0:T(1024)(128)(4,1)S(1)}, s32[]{:S(2)}) async-start(s8[6291456]{0:T(1024)(128)(4,1)} %bitcast.125), calls=%async_computation.7 | async-start | bytes 8388608
  164.8 28.6 %slice-start.8 = ((s8[6291456]{0:T(1024)(128)(4,1)}), s8[2097152]{0:T(1024)(128)(4,1)S(1)}, s32[]{:S(2)}) async-start(s8[6291456]{0:T(1024)(128)(4,1)} %bitcast.125), calls=%async_computation.8 | async-start | bytes 4194304
  164.8 23.9 %collective-permute-start.4 = (f32[2,8,128,128]{2,3,0,1:T(8,128)}, f32[2,8,128,128]{2,3,0,1:T(8,128)}, u32[]{:S(2)}, u32[]{:S(2)}) collective-permute-start(f32[2,8,128,128]{2,3,0,1:T(8,128)} %slice_add_fusion), channel_id=1, source_target_pairs={{0,8},{8,0},{4,12},{12,4},{16,24},{24,16},{20,28},{28,20},{1,9},{9... | collective-permute-start | bytes 3145736 | tf_op jit(solution)/shard_map/ppermute | solution.py:18
  190.0 47.9 %collective-permute-start.5 = (f32[1,8,128,128]{2,3,0,1:T(8,128)S(1)}, f32[1,8,128,128]{2,3,0,1:T(8,128)}, u32[]{:S(2)}, u32[]{:S(2)}) collective-permute-start(f32[1,8,128,128]{2,3,0,1:T(8,128)S(1)} %slice_add_fusion.1), channel_id=1, source_target_pairs={{0,16},{16,0},{4,20},{20,4},{8,24},{24,8},{12,28},{28,12},{1,17},{... | collective-permute-start | bytes 1572872 | tf_op jit(solution)/shard_map/ppermute | solution.py:18
